TPU v7x, 256 devices: a whole 4x4x8 slice. The times are simulated.
256 devices in a mesh: tm: 16 (over z, core), space: 16 (over x, y).
Axes of the slice: x: 4, y: 4, z: 8, core: 2. Of those that a mesh axis runs over, the one named last changes fastest.
Arguments:
- initial_state: float32 [128, 128, 128], P('space'), may hold values from -1 to 1
- fine_steps: int32 [16], P('tm'), may hold values from 2 to 8, as said below
- sweep_count: int32 [1], replicated, may hold values from 2 to 4
Outputs:
- end_states: float32 [16, 128, 128, 128], P('tm', 'space')
Inputs may be any that keep to these rules, and one draw needn't show every extreme that they name: Slice n takes fine_steps[n] fine steps; some slice takes exactly 8.
All inputs are finite; a program needn't handle non-finite values.
Results may differ from a plain program's by a relative error of at most 0.0001.
Values sent between devices are 32-bit elements; how exact they have to be, the bound alone decides.
A program may use at most 64 MiB of HBM per device.

v0:
```python
import jax
import jax.numpy as jnp
from jax import lax
from jax.sharding import PartitionSpec as P

FSTEPS = 8
PITERS = 2


SLICE_TIME = 0.6
MOBILITY = 0.5


def extended_2(cells, sides, width):
    for axis, dim in sides:
        count = lax.axis_size(axis)
        head = lax.slice_in_dim(cells, 0, width, axis=dim)
        tail = lax.slice_in_dim(cells, cells.shape[dim] - width, cells.shape[dim], axis=dim)
        cells = jnp.concatenate(
            [
                lax.ppermute(tail, axis, [(i, (i + 1) % count) for i in range(count)]),
                cells,
                lax.ppermute(head, axis, [((i + 1) % count, i) for i in range(count)]),
            ],
            axis=dim,
        )
    return cells


def shifted(block, axis, distance):
    devices = range(lax.axis_size(axis))
    route = [(i - distance, i) for i in devices if i - distance in devices]
    return lax.ppermute(block, axis, route)


def planar_sum(field):
    return (
        jnp.roll(field, 1, 1)
        + jnp.roll(field, -1, 1)
        + jnp.roll(field, 1, 2)
        + jnp.roll(field, -1, 2)
    )


def coarse(state, sweeps):
    source = state + SLICE_TIME * (state - state * state * state)
    weight = SLICE_TIME * MOBILITY
    divisor = 1.0 + 4.0 * weight

    def sweep(turn, guess):
        return (source + weight * planar_sum(guess)) / divisor

    return lax.fori_loop(0, sweeps, sweep, source)


def advance(extended, step_size, active):
    center = extended[1:-1]
    neighbours = extended[2:] + extended[:-2] + planar_sum(center)
    moved = center + step_size * (
        MOBILITY * (neighbours - 6.0 * center) + center - center * center * center
    )
    return jnp.where(active, moved, center)


def fine_solve(state, step_count):
    step_size = SLICE_TIME / step_count.astype(jnp.float32)

    def single(turn, field):
        extended = extended_2(field, (("space", 0),), 1)
        return advance(extended, step_size, turn < step_count)

    return lax.fori_loop(0, FSTEPS, single, state)


def local(initial_state, fine_steps, sweep_count):
    position = lax.axis_index("tm")
    length = lax.axis_size("tm")
    sweeps = sweep_count[0]
    step_count = fine_steps[0]

    def repeat(turn, current):
        return jnp.where(turn < position, coarse(current, sweeps), current)

    start = lax.fori_loop(0, length - 1, repeat, initial_state)
    final = start
    for outer_round in range(PITERS):
        correction = fine_solve(start, step_count) - coarse(start, sweeps)

        def relay(turn, current):
            moved = shifted(coarse(current, sweeps) + correction, "tm", 1)
            return jnp.where(position == 0, initial_state, moved)

        start = lax.fori_loop(0, length - 1, relay, start)
        final = coarse(start, sweeps) + correction
    return final[None]


def solution(mesh):
    placed = (P("space", None, None), P("tm"), P())
    return jax.shard_map(
        local, mesh=mesh, in_specs=placed, out_specs=P("tm", "space", None, None), check_vma=False
    )
```

profile of v0, /device:TPU:128, one launch (start us, length us, event | category | flops | bytes accessed | tf_op | source)
XLA Modules:
  0.0 896.4 jit_solution(9426852856052771472)
XLA Ops:
  1.0 110.3 %while.148 = (s32[]{:T(128)}, f32[8,128,128]{2,1,0:T(8,128)S(1)}, s32[]{:T(128)}, s32[]{:T(128)}, s32[]{:T(128)}, /*index=5*/s32[]{:T(128)}, s32[]{:T(128)}) while((s32[]{:T(128)}, f32[8,128,128]{2,1,0:T(8,128)S(1)}, s32[]{:T(128)}, s32[]{:T(128)}, s32[]{:T(128)}, /*index=5*/s32[]{:T(128)}, s32[]{:T(128)}) %tuple.339), condition=%wide.region_3.4_spmd, body=%wide.region_0.3_spmd.sunk | while | flops 2097157 | bytes 11010252 | solution.py:84
  1.2 7.1 while.158
  8.5 7.1 while.158
  15.9 7.1 while.158
  23.2 7.1 while.158
  30.6 7.1 while.158
  37.9 7.1 while.158
  45.3 7.1 while.158
  52.6 7.1 while.158
  60.0 7.1 while.158
  67.4 7.1 while.158
  74.7 7.1 while.158
  82.1 7.1 while.158
  89.4 7.1 while.158
  96.8 7.1 while.158
  104.1 7.1 while.158
  112.9 90.3 %while.149 = (s32[]{:T(128)}, f32[8,128,128]{2,1,0:T(8,128)}, s32[]{:T(128)}, f32[]{:T(128)}, s32[]{:T(128)}) while((s32[]{:T(128)}, f32[8,128,128]{2,1,0:T(8,128)}, s32[]{:T(128)}, f32[]{:T(128)}, s32[]{:T(128)}) %tuple.315), condition=%wide.region_5.6_spmd, body=%wide.region_4.5_spmd.sunk | while | flops 2752515 | bytes 9306275 | solution.py:72
  203.3 7.1 while.150
  211.7 285.8 %while.152 = (s32[]{:T(128)}, f32[8,128,128]{2,1,0:T(8,128)S(1)}, pred[]{:T(512)}, s32[]{:T(128)}, f32[8,128,128]{2,1,0:T(8,128)S(1)}, /*index=5*/f32[8,128,128]{2,1,0:T(8,128)S(1)}, s32[]{:T(128)}, s32[]{:T(128)}, s32[]{:T(128)}) while((s32[]{:T(128)}, f32[8,128,128]{2,1,0:T(8,128)S(1)}, pred[]{:T(512)}, s32[]{:T(128)}, ...), condition=%wide.region_11.12_spmd, body=%wide.region_8.11_spmd.sunk | while | flops 2228228 | bytes 14680307 | solution.py:93
  220.9 9.8 %collective-permute-done.5 = f32[8,128,128]{2,1,0:T(8,128)S(1)} collective-permute-done((f32[8,128,128]{2,1,0:T(8,128)S(1)}, f32[8,128,128]{2,1,0:T(8,128)S(1)}, u32[]{:S(2)}, u32[]{:S(2)}) %collective-permute-start.5) | collective-permute-done | bytes 524320 | tf_op jit(solution)/shard_map/while/body/eval_jaxpr/ppermute | solution.py:33
  239.9 9.8 %collective-permute-done.5 = f32[8,128,128]{2,1,0:T(8,128)S(1)} collective-permute-done((f32[8,128,128]{2,1,0:T(8,128)S(1)}, f32[8,128,128]{2,1,0:T(8,128)S(1)}, u32[]{:S(2)}, u32[]{:S(2)}) %collective-permute-start.5) | collective-permute-done | bytes 524320 | tf_op jit(solution)/shard_map/while/body/eval_jaxpr/ppermute | solution.py:33
  259.0 9.8 %collective-permute-done.5 = f32[8,128,128]{2,1,0:T(8,128)S(1)} collective-permute-done((f32[8,128,128]{2,1,0:T(8,128)S(1)}, f32[8,128,128]{2,1,0:T(8,128)S(1)}, u32[]{:S(2)}, u32[]{:S(2)}) %collective-permute-start.5) | collective-permute-done | bytes 524320 | tf_op jit(solution)/shard_map/while/body/eval_jaxpr/ppermute | solution.py:33
  278.0 9.8 %collective-permute-done.5 = f32[8,128,128]{2,1,0:T(8,128)S(1)} collective-permute-done((f32[8,128,128]{2,1,0:T(8,128)S(1)}, f32[8,128,128]{2,1,0:T(8,128)S(1)}, u32[]{:S(2)}, u32[]{:S(2)}) %collective-permute-start.5) | collective-permute-done | bytes 524320 | tf_op jit(solution)/shard_map/while/body/eval_jaxpr/ppermute | solution.py:33
  297.1 9.8 %collective-permute-done.5 = f32[8,128,128]{2,1,0:T(8,128)S(1)} collective-permute-done((f32[8,128,128]{2,1,0:T(8,128)S(1)}, f32[8,128,128]{2,1,0:T(8,128)S(1)}, u32[]{:S(2)}, u32[]{:S(2)}) %collective-permute-start.5) | collective-permute-done | bytes 524320 | tf_op jit(solution)/shard_map/while/body/eval_jaxpr/ppermute | solution.py:33
  307.1 7.0 while.159
  316.1 9.8 %collective-permute-done.5 = f32[8,128,128]{2,1,0:T(8,128)S(1)} collective-permute-done((f32[8,128,128]{2,1,0:T(8,128)S(1)}, f32[8,128,128]{2,1,0:T(8,128)S(1)}, u32[]{:S(2)}, u32[]{:S(2)}) %collective-permute-start.5) | collective-permute-done | bytes 524320 | tf_op jit(solution)/shard_map/while/body/eval_jaxpr/ppermute | solution.py:33
  326.1 7.0 while.159
  335.2 9.8 %collective-permute-done.5 = f32[8,128,128]{2,1,0:T(8,128)S(1)} collective-permute-done((f32[8,128,128]{2,1,0:T(8,128)S(1)}, f32[8,128,128]{2,1,0:T(8,128)S(1)}, u32[]{:S(2)}, u32[]{:S(2)}) %collective-permute-start.5) | collective-permute-done | bytes 524320 | tf_op jit(solution)/shard_map/while/body/eval_jaxpr/ppermute | solution.py:33
  345.2 7.0 while.159
  354.2 9.8 %collective-permute-done.5 = f32[8,128,128]{2,1,0:T(8,128)S(1)} collective-permute-done((f32[8,128,128]{2,1,0:T(8,128)S(1)}, f32[8,128,128]{2,1,0:T(8,128)S(1)}, u32[]{:S(2)}, u32[]{:S(2)}) %collective-permute-start.5) | collective-permute-done | bytes 524320 | tf_op jit(solution)/shard_map/while/body/eval_jaxpr/ppermute | solution.py:33
  364.2 7.0 while.159
  373.3 9.8 %collective-permute-done.5 = f32[8,128,128]{2,1,0:T(8,128)S(1)} collective-permute-done((f32[8,128,128]{2,1,0:T(8,128)S(1)}, f32[8,128,128]{2,1,0:T(8,128)S(1)}, u32[]{:S(2)}, u32[]{:S(2)}) %collective-permute-start.5) | collective-permute-done | bytes 524320 | tf_op jit(solution)/shard_map/while/body/eval_jaxpr/ppermute | solution.py:33
  383.3 7.0 while.159
  392.3 9.8 %collective-permute-done.5 = f32[8,128,128]{2,1,0:T(8,128)S(1)} collective-permute-done((f32[8,128,128]{2,1,0:T(8,128)S(1)}, f32[8,128,128]{2,1,0:T(8,128)S(1)}, u32[]{:S(2)}, u32[]{:S(2)}) %collective-permute-start.5) | collective-permute-done | bytes 524320 | tf_op jit(solution)/shard_map/while/body/eval_jaxpr/ppermute | solution.py:33
  402.3 7.0 while.159
  411.4 9.8 %collective-permute-done.5 = f32[8,128,128]{2,1,0:T(8,128)S(1)} collective-permute-done((f32[8,128,128]{2,1,0:T(8,128)S(1)}, f32[8,128,128]{2,1,0:T(8,128)S(1)}, u32[]{:S(2)}, u32[]{:S(2)}) %collective-permute-start.5) | collective-permute-done | bytes 524320 | tf_op jit(solution)/shard_map/while/body/eval_jaxpr/ppermute | solution.py:33
  421.4 7.0 while.159
  430.4 9.8 %collective-permute-done.5 = f32[8,128,128]{2,1,0:T(8,128)S(1)} collective-permute-done((f32[8,128,128]{2,1,0:T(8,128)S(1)}, f32[8,128,128]{2,1,0:T(8,128)S(1)}, u32[]{:S(2)}, u32[]{:S(2)}) %collective-permute-start.5) | collective-permute-done | bytes 524320 | tf_op jit(solution)/shard_map/while/body/eval_jaxpr/ppermute | solution.py:33
  440.4 7.0 while.159
  449.5 9.8 %collective-permute-done.5 = f32[8,128,128]{2,1,0:T(8,128)S(1)} collective-permute-done((f32[8,128,128]{2,1,0:T(8,128)S(1)}, f32[8,128,128]{2,1,0:T(8,128)S(1)}, u32[]{:S(2)}, u32[]{:S(2)}) %collective-permute-start.5) | collective-permute-done | bytes 524320 | tf_op jit(solution)/shard_map/while/body/eval_jaxpr/ppermute | solution.py:33
  468.6 9.8 %collective-permute-done.5 = f32[8,128,128]{2,1,0:T(8,128)S(1)} collective-permute-done((f32[8,128,128]{2,1,0:T(8,128)S(1)}, f32[8,128,128]{2,1,0:T(8,128)S(1)}, u32[]{:S(2)}, u32[]{:S(2)}) %collective-permute-start.5) | collective-permute-done | bytes 524320 | tf_op jit(solution)/shard_map/while/body/eval_jaxpr/ppermute | solution.py:33
  487.6 9.8 %collective-permute-done.5 = f32[8,128,128]{2,1,0:T(8,128)S(1)} collective-permute-done((f32[8,128,128]{2,1,0:T(8,128)S(1)}, f32[8,128,128]{2,1,0:T(8,128)S(1)}, u32[]{:S(2)}, u32[]{:S(2)}) %collective-permute-start.5) | collective-permute-done | bytes 524320 | tf_op jit(solution)/shard_map/while/body/eval_jaxpr/ppermute | solution.py:33
  498.2 95.9 %while.153 = (s32[]{:T(128)}, f32[8,128,128]{2,1,0:T(8,128)}, s32[]{:T(128)}, f32[]{:T(128)}, s32[]{:T(128)}) while((s32[]{:T(128)}, f32[8,128,128]{2,1,0:T(8,128)}, s32[]{:T(128)}, f32[]{:T(128)}, s32[]{:T(128)}) %tuple.324), condition=%wide.region_13.14_spmd, body=%wide.region_12.13_spmd.sunk | while | flops 2752515 | bytes 9306275 | solution.py:72
  594.3 7.1 while.154
  602.5 285.8 %while.156 = (s32[]{:T(128)}, f32[8,128,128]{2,1,0:T(8,128)S(1)}, pred[]{:T(512)}, s32[]{:T(128)}, f32[8,128,128]{2,1,0:T(8,128)S(1)}, /*index=5*/f32[8,128,128]{2,1,0:T(8,128)S(1)}, s32[]{:T(128)}, s32[]{:T(128)}, s32[]{:T(128)}) while((s32[]{:T(128)}, f32[8,128,128]{2,1,0:T(8,128)S(1)}, pred[]{:T(512)}, s32[]{:T(128)}, ...), condition=%wide.region_19.20_spmd, body=%wide.region_16.19_spmd.sunk | while | flops 2228228 | bytes 14680307 | solution.py:93
  611.7 9.8 %collective-permute-done.4 = f32[8,128,128]{2,1,0:T(8,128)S(1)} collective-permute-done((f32[8,128,128]{2,1,0:T(8,128)S(1)}, f32[8,128,128]{2,1,0:T(8,128)S(1)}, u32[]{:S(2)}, u32[]{:S(2)}) %collective-permute-start.4) | collective-permute-done | bytes 524320 | tf_op jit(solution)/shard_map/while/body/eval_jaxpr/ppermute | solution.py:33
  630.8 9.8 %collective-permute-done.4 = f32[8,128,128]{2,1,0:T(8,128)S(1)} collective-permute-done((f32[8,128,128]{2,1,0:T(8,128)S(1)}, f32[8,128,128]{2,1,0:T(8,128)S(1)}, u32[]{:S(2)}, u32[]{:S(2)}) %collective-permute-start.4) | collective-permute-done | bytes 524320 | tf_op jit(solution)/shard_map/while/body/eval_jaxpr/ppermute | solution.py:33
  649.8 9.8 %collective-permute-done.4 = f32[8,128,128]{2,1,0:T(8,128)S(1)} collective-permute-done((f32[8,128,128]{2,1,0:T(8,128)S(1)}, f32[8,128,128]{2,1,0:T(8,128)S(1)}, u32[]{:S(2)}, u32[]{:S(2)}) %collective-permute-start.4) | collective-permute-done | bytes 524320 | tf_op jit(solution)/shard_map/while/body/eval_jaxpr/ppermute | solution.py:33
  668.9 9.8 %collective-permute-done.4 = f32[8,128,128]{2,1,0:T(8,128)S(1)} collective-permute-done((f32[8,128,128]{2,1,0:T(8,128)S(1)}, f32[8,128,128]{2,1,0:T(8,128)S(1)}, u32[]{:S(2)}, u32[]{:S(2)}) %collective-permute-start.4) | collective-permute-done | bytes 524320 | tf_op jit(solution)/shard_map/while/body/eval_jaxpr/ppermute | solution.py:33
  687.9 9.8 %collective-permute-done.4 = f32[8,128,128]{2,1,0:T(8,128)S(1)} collective-permute-done((f32[8,128,128]{2,1,0:T(8,128)S(1)}, f32[8,128,128]{2,1,0:T(8,128)S(1)}, u32[]{:S(2)}, u32[]{:S(2)}) %collective-permute-start.4) | collective-permute-done | bytes 524320 | tf_op jit(solution)/shard_map/while/body/eval_jaxpr/ppermute | solution.py:33
  707.0 9.8 %collective-permute-done.4 = f32[8,128,128]{2,1,0:T(8,128)S(1)} collective-permute-done((f32[8,128,128]{2,1,0:T(8,128)S(1)}, f32[8,128,128]{2,1,0:T(8,128)S(1)}, u32[]{:S(2)}, u32[]{:S(2)}) %collective-permute-start.4) | collective-permute-done | bytes 524320 | tf_op jit(solution)/shard_map/while/body/eval_jaxpr/ppermute | solution.py:33
  726.0 9.8 %collective-permute-done.4 = f32[8,128,128]{2,1,0:T(8,128)S(1)} collective-permute-done((f32[8,128,128]{2,1,0:T(8,128)S(1)}, f32[8,128,128]{2,1,0:T(8,128)S(1)}, u32[]{:S(2)}, u32[]{:S(2)}) %collective-permute-start.4) | collective-permute-done | bytes 524320 | tf_op jit(solution)/shard_map/while/body/eval_jaxpr/ppermute | solution.py:33
  745.1 9.8 %collective-permute-done.4 = f32[8,128,128]{2,1,0:T(8,128)S(1)} collective-permute-done((f32[8,128,128]{2,1,0:T(8,128)S(1)}, f32[8,128,128]{2,1,0:T(8,128)S(1)}, u32[]{:S(2)}, u32[]{:S(2)}) %collective-permute-start.4) | collective-permute-done | bytes 524320 | tf_op jit(solution)/shard_map/while/body/eval_jaxpr/ppermute | solution.py:33
  764.1 9.8 %collective-permute-done.4 = f32[8,128,128]{2,1,0:T(8,128)S(1)} collective-permute-done((f32[8,128,128]{2,1,0:T(8,128)S(1)}, f32[8,128,128]{2,1,0:T(8,128)S(1)}, u32[]{:S(2)}, u32[]{:S(2)}) %collective-permute-start.4) | collective-permute-done | bytes 524320 | tf_op jit(solution)/shard_map/while/body/eval_jaxpr/ppermute | solution.py:33
  774.1 7.0 while.160
  783.2 9.8 %collective-permute-done.4 = f32[8,128,128]{2,1,0:T(8,128)S(1)} collective-permute-done((f32[8,128,128]{2,1,0:T(8,128)S(1)}, f32[8,128,128]{2,1,0:T(8,128)S(1)}, u32[]{:S(2)}, u32[]{:S(2)}) %collective-permute-start.4) | collective-permute-done | bytes 524320 | tf_op jit(solution)/shard_map/while/body/eval_jaxpr/ppermute | solution.py:33
  793.2 7.0 while.160
  802.2 9.8 %collective-permute-done.4 = f32[8,128,128]{2,1,0:T(8,128)S(1)} collective-permute-done((f32[8,128,128]{2,1,0:T(8,128)S(1)}, f32[8,128,128]{2,1,0:T(8,128)S(1)}, u32[]{:S(2)}, u32[]{:S(2)}) %collective-permute-start.4) | collective-permute-done | bytes 524320 | tf_op jit(solution)/shard_map/while/body/eval_jaxpr/ppermute | solution.py:33
  812.3 7.0 while.160
  821.3 9.8 %collective-permute-done.4 = f32[8,128,128]{2,1,0:T(8,128)S(1)} collective-permute-done((f32[8,128,128]{2,1,0:T(8,128)S(1)}, f32[8,128,128]{2,1,0:T(8,128)S(1)}, u32[]{:S(2)}, u32[]{:S(2)}) %collective-permute-start.4) | collective-permute-done | bytes 524320 | tf_op jit(solution)/shard_map/while/body/eval_jaxpr/ppermute | solution.py:33
  831.3 7.0 while.160
  840.4 9.8 %collective-permute-done.4 = f32[8,128,128]{2,1,0:T(8,128)S(1)} collective-permute-done((f32[8,128,128]{2,1,0:T(8,128)S(1)}, f32[8,128,128]{2,1,0:T(8,128)S(1)}, u32[]{:S(2)}, u32[]{:S(2)}) %collective-permute-start.4) | collective-permute-done | bytes 524320 | tf_op jit(solution)/shard_map/while/body/eval_jaxpr/ppermute | solution.py:33
  859.4 9.8 %collective-permute-done.4 = f32[8,128,128]{2,1,0:T(8,128)S(1)} collective-permute-done((f32[8,128,128]{2,1,0:T(8,128)S(1)}, f32[8,128,128]{2,1,0:T(8,128)S(1)}, u32[]{:S(2)}, u32[]{:S(2)}) %collective-permute-start.4) | collective-permute-done | bytes 524320 | tf_op jit(solution)/shard_map/while/body/eval_jaxpr/ppermute | solution.py:33
  878.5 9.8 %collective-permute-done.4 = f32[8,128,128]{2,1,0:T(8,128)S(1)} collective-permute-done((f32[8,128,128]{2,1,0:T(8,128)S(1)}, f32[8,128,128]{2,1,0:T(8,128)S(1)}, u32[]{:S(2)}, u32[]{:S(2)}) %collective-permute-start.4) | collective-permute-done | bytes 524320 | tf_op jit(solution)/shard_map/while/body/eval_jaxpr/ppermute | solution.py:33
  (1369 shorter events, 560.0 us)
Async XLA Ops:
  111.3 91.8 %copy-start.1 = (f32[8,128,128]{2,1,0:T(8,128)}, f32[8,128,128]{2,1,0:T(8,128)S(1)}, u32[]{:S(2)}) copy-start(f32[8,128,128]{2,1,0:T(8,128)S(1)} %get-tuple-element.1267) | copy-start | bytes 1572868
  113.9 7.7 collective-permute-start
  115.6 6.0 collective-permute-start.1
  125.1 7.7 collective-permute-start
  125.2 7.6 collective-permute-start.1
  136.4 7.8 collective-permute-start
  136.4 7.7 collective-permute-start.1
  147.7 7.8 collective-permute-start
  147.8 7.7 collective-permute-start.1
  159.0 7.8 collective-permute-start
  159.1 7.7 collective-permute-start.1
  170.3 7.8 collective-permute-start
  170.4 7.7 collective-permute-start.1
  181.6 7.8 collective-permute-start
  181.7 7.7 collective-permute-start.1
  192.9 7.8 collective-permute-start
  193.0 7.7 collective-permute-start.1
  210.3 1.4 copy-start.2
  219.0 11.7 %collective-permute-start.5 = (f32[8,128,128]{2,1,0:T(8,128)S(1)}, f32[8,128,128]{2,1,0:T(8,128)S(1)}, u32[]{:S(2)}, u32[]{:S(2)}) collective-permute-start(f32[8,128,128]{2,1,0:T(8,128)S(1)} %add.625), channel_id=1, source_target_pairs={{0,16},{16,32},{32,48},{48,64},{64,80},{80,96},{96,112},{112,128},... | collective-permute-start | bytes 1572872 | tf_op jit(solution)/shard_map/while/body/eval_jaxpr/ppermute | solution.py:33
  238.0 11.7 %collective-permute-start.5 = (f32[8,128,128]{2,1,0:T(8,128)S(1)}, f32[8,128,128]{2,1,0:T(8,128)S(1)}, u32[]{:S(2)}, u32[]{:S(2)}) collective-permute-start(f32[8,128,128]{2,1,0:T(8,128)S(1)} %add.625), channel_id=1, source_target_pairs={{0,16},{16,32},{32,48},{48,64},{64,80},{80,96},{96,112},{112,128},... | collective-permute-start | bytes 1572872 | tf_op jit(solution)/shard_map/while/body/eval_jaxpr/ppermute | solution.py:33
  257.1 11.7 %collective-permute-start.5 = (f32[8,128,128]{2,1,0:T(8,128)S(1)}, f32[8,128,128]{2,1,0:T(8,128)S(1)}, u32[]{:S(2)}, u32[]{:S(2)}) collective-permute-start(f32[8,128,128]{2,1,0:T(8,128)S(1)} %add.625), channel_id=1, source_target_pairs={{0,16},{16,32},{32,48},{48,64},{64,80},{80,96},{96,112},{112,128},... | collective-permute-start | bytes 1572872 | tf_op jit(solution)/shard_map/while/body/eval_jaxpr/ppermute | solution.py:33
  276.1 11.7 %collective-permute-start.5 = (f32[8,128,128]{2,1,0:T(8,128)S(1)}, f32[8,128,128]{2,1,0:T(8,128)S(1)}, u32[]{:S(2)}, u32[]{:S(2)}) collective-permute-start(f32[8,128,128]{2,1,0:T(8,128)S(1)} %add.625), channel_id=1, source_target_pairs={{0,16},{16,32},{32,48},{48,64},{64,80},{80,96},{96,112},{112,128},... | collective-permute-start | bytes 1572872 | tf_op jit(solution)/shard_map/while/body/eval_jaxpr/ppermute | solution.py:33
  295.2 11.7 %collective-permute-start.5 = (f32[8,128,128]{2,1,0:T(8,128)S(1)}, f32[8,128,128]{2,1,0:T(8,128)S(1)}, u32[]{:S(2)}, u32[]{:S(2)}) collective-permute-start(f32[8,128,128]{2,1,0:T(8,128)S(1)} %add.625), channel_id=1, source_target_pairs={{0,16},{16,32},{32,48},{48,64},{64,80},{80,96},{96,112},{112,128},... | collective-permute-start | bytes 1572872 | tf_op jit(solution)/shard_map/while/body/eval_jaxpr/ppermute | solution.py:33
  314.2 11.7 %collective-permute-start.5 = (f32[8,128,128]{2,1,0:T(8,128)S(1)}, f32[8,128,128]{2,1,0:T(8,128)S(1)}, u32[]{:S(2)}, u32[]{:S(2)}) collective-permute-start(f32[8,128,128]{2,1,0:T(8,128)S(1)} %add.625), channel_id=1, source_target_pairs={{0,16},{16,32},{32,48},{48,64},{64,80},{80,96},{96,112},{112,128},... | collective-permute-start | bytes 1572872 | tf_op jit(solution)/shard_map/while/body/eval_jaxpr/ppermute | solution.py:33
  333.3 11.7 %collective-permute-start.5 = (f32[8,128,128]{2,1,0:T(8,128)S(1)}, f32[8,128,128]{2,1,0:T(8,128)S(1)}, u32[]{:S(2)}, u32[]{:S(2)}) collective-permute-start(f32[8,128,128]{2,1,0:T(8,128)S(1)} %add.625), channel_id=1, source_target_pairs={{0,16},{16,32},{32,48},{48,64},{64,80},{80,96},{96,112},{112,128},... | collective-permute-start | bytes 1572872 | tf_op jit(solution)/shard_map/while/body/eval_jaxpr/ppermute | solution.py:33
  352.3 11.7 %collective-permute-start.5 = (f32[8,128,128]{2,1,0:T(8,128)S(1)}, f32[8,128,128]{2,1,0:T(8,128)S(1)}, u32[]{:S(2)}, u32[]{:S(2)}) collective-permute-start(f32[8,128,128]{2,1,0:T(8,128)S(1)} %add.625), channel_id=1, source_target_pairs={{0,16},{16,32},{32,48},{48,64},{64,80},{80,96},{96,112},{112,128},... | collective-permute-start | bytes 1572872 | tf_op jit(solution)/shard_map/while/body/eval_jaxpr/ppermute | solution.py:33
  371.4 11.7 %collective-permute-start.5 = (f32[8,128,128]{2,1,0:T(8,128)S(1)}, f32[8,128,128]{2,1,0:T(8,128)S(1)}, u32[]{:S(2)}, u32[]{:S(2)}) collective-permute-start(f32[8,128,128]{2,1,0:T(8,128)S(1)} %add.625), channel_id=1, source_target_pairs={{0,16},{16,32},{32,48},{48,64},{64,80},{80,96},{96,112},{112,128},... | collective-permute-start | bytes 1572872 | tf_op jit(solution)/shard_map/while/body/eval_jaxpr/ppermute | solution.py:33
  390.4 11.7 %collective-permute-start.5 = (f32[8,128,128]{2,1,0:T(8,128)S(1)}, f32[8,128,128]{2,1,0:T(8,128)S(1)}, u32[]{:S(2)}, u32[]{:S(2)}) collective-permute-start(f32[8,128,128]{2,1,0:T(8,128)S(1)} %add.625), channel_id=1, source_target_pairs={{0,16},{16,32},{32,48},{48,64},{64,80},{80,96},{96,112},{112,128},... | collective-permute-start | bytes 1572872 | tf_op jit(solution)/shard_map/while/body/eval_jaxpr/ppermute | solution.py:33
  409.5 11.7 %collective-permute-start.5 = (f32[8,128,128]{2,1,0:T(8,128)S(1)}, f32[8,128,128]{2,1,0:T(8,128)S(1)}, u32[]{:S(2)}, u32[]{:S(2)}) collective-permute-start(f32[8,128,128]{2,1,0:T(8,128)S(1)} %add.625), channel_id=1, source_target_pairs={{0,16},{16,32},{32,48},{48,64},{64,80},{80,96},{96,112},{112,128},... | collective-permute-start | bytes 1572872 | tf_op jit(solution)/shard_map/while/body/eval_jaxpr/ppermute | solution.py:33
  428.5 11.7 %collective-permute-start.5 = (f32[8,128,128]{2,1,0:T(8,128)S(1)}, f32[8,128,128]{2,1,0:T(8,128)S(1)}, u32[]{:S(2)}, u32[]{:S(2)}) collective-permute-start(f32[8,128,128]{2,1,0:T(8,128)S(1)} %add.625), channel_id=1, source_target_pairs={{0,16},{16,32},{32,48},{48,64},{64,80},{80,96},{96,112},{112,128},... | collective-permute-start | bytes 1572872 | tf_op jit(solution)/shard_map/while/body/eval_jaxpr/ppermute | solution.py:33
  447.6 11.7 %collective-permute-start.5 = (f32[8,128,128]{2,1,0:T(8,128)S(1)}, f32[8,128,128]{2,1,0:T(8,128)S(1)}, u32[]{:S(2)}, u32[]{:S(2)}) collective-permute-start(f32[8,128,128]{2,1,0:T(8,128)S(1)} %add.625), channel_id=1, source_target_pairs={{0,16},{16,32},{32,48},{48,64},{64,80},{80,96},{96,112},{112,128},... | collective-permute-start | bytes 1572872 | tf_op jit(solution)/shard_map/while/body/eval_jaxpr/ppermute | solution.py:33
  466.6 11.7 %collective-permute-start.5 = (f32[8,128,128]{2,1,0:T(8,128)S(1)}, f32[8,128,128]{2,1,0:T(8,128)S(1)}, u32[]{:S(2)}, u32[]{:S(2)}) collective-permute-start(f32[8,128,128]{2,1,0:T(8,128)S(1)} %add.625), channel_id=1, source_target_pairs={{0,16},{16,32},{32,48},{48,64},{64,80},{80,96},{96,112},{112,128},... | collective-permute-start | bytes 1572872 | tf_op jit(solution)/shard_map/while/body/eval_jaxpr/ppermute | solution.py:33
  485.7 11.7 %collective-permute-start.5 = (f32[8,128,128]{2,1,0:T(8,128)S(1)}, f32[8,128,128]{2,1,0:T(8,128)S(1)}, u32[]{:S(2)}, u32[]{:S(2)}) collective-permute-start(f32[8,128,128]{2,1,0:T(8,128)S(1)} %add.625), channel_id=1, source_target_pairs={{0,16},{16,32},{32,48},{48,64},{64,80},{80,96},{96,112},{112,128},... | collective-permute-start | bytes 1572872 | tf_op jit(solution)/shard_map/while/body/eval_jaxpr/ppermute | solution.py:33
  499.3 8.4 collective-permute-start.2
  499.4 8.3 collective-permute-start.3
  511.4 8.2 collective-permute-start.2
  511.5 8.2 collective-permute-start.3
  523.4 8.2 collective-permute-start.2
  523.5 8.2 collective-permute-start.3
  535.3 8.2 collective-permute-start.2
  535.4 8.2 collective-permute-start.3
  547.3 8.2 collective-permute-start.2
  547.4 8.2 collective-permute-start.3
  559.2 8.4 collective-permute-start.2
  559.3 8.3 collective-permute-start.3
  571.3 8.2 collective-permute-start.2
  571.4 8.2 collective-permute-start.3
  583.3 8.2 collective-permute-start.2
  583.3 8.2 collective-permute-start.3
  609.8 11.7 %collective-permute-start.4 = (f32[8,128,128]{2,1,0:T(8,128)S(1)}, f32[8,128,128]{2,1,0:T(8,128)S(1)}, u32[]{:S(2)}, u32[]{:S(2)}) collective-permute-start(f32[8,128,128]{2,1,0:T(8,128)S(1)} %add.641), channel_id=1, source_target_pairs={{0,16},{16,32},{32,48},{48,64},{64,80},{80,96},{96,112},{112,128},... | collective-permute-start | bytes 1572872 | tf_op jit(solution)/shard_map/while/body/eval_jaxpr/ppermute | solution.py:33
  628.9 11.7 %collective-permute-start.4 = (f32[8,128,128]{2,1,0:T(8,128)S(1)}, f32[8,128,128]{2,1,0:T(8,128)S(1)}, u32[]{:S(2)}, u32[]{:S(2)}) collective-permute-start(f32[8,128,128]{2,1,0:T(8,128)S(1)} %add.641), channel_id=1, source_target_pairs={{0,16},{16,32},{32,48},{48,64},{64,80},{80,96},{96,112},{112,128},... | collective-permute-start | bytes 1572872 | tf_op jit(solution)/shard_map/while/body/eval_jaxpr/ppermute | solution.py:33
  647.9 11.7 %collective-permute-start.4 = (f32[8,128,128]{2,1,0:T(8,128)S(1)}, f32[8,128,128]{2,1,0:T(8,128)S(1)}, u32[]{:S(2)}, u32[]{:S(2)}) collective-permute-start(f32[8,128,128]{2,1,0:T(8,128)S(1)} %add.641), channel_id=1, source_target_pairs={{0,16},{16,32},{32,48},{48,64},{64,80},{80,96},{96,112},{112,128},... | collective-permute-start | bytes 1572872 | tf_op jit(solution)/shard_map/while/body/eval_jaxpr/ppermute | solution.py:33
  667.0 11.7 %collective-permute-start.4 = (f32[8,128,128]{2,1,0:T(8,128)S(1)}, f32[8,128,128]{2,1,0:T(8,128)S(1)}, u32[]{:S(2)}, u32[]{:S(2)}) collective-permute-start(f32[8,128,128]{2,1,0:T(8,128)S(1)} %add.641), channel_id=1, source_target_pairs={{0,16},{16,32},{32,48},{48,64},{64,80},{80,96},{96,112},{112,128},... | collective-permute-start | bytes 1572872 | tf_op jit(solution)/shard_map/while/body/eval_jaxpr/ppermute | solution.py:33
  686.0 11.7 %collective-permute-start.4 = (f32[8,128,128]{2,1,0:T(8,128)S(1)}, f32[8,128,128]{2,1,0:T(8,128)S(1)}, u32[]{:S(2)}, u32[]{:S(2)}) collective-permute-start(f32[8,128,128]{2,1,0:T(8,128)S(1)} %add.641), channel_id=1, source_target_pairs={{0,16},{16,32},{32,48},{48,64},{64,80},{80,96},{96,112},{112,128},... | collective-permute-start | bytes 1572872 | tf_op jit(solution)/shard_map/while/body/eval_jaxpr/ppermute | solution.py:33
  705.1 11.7 %collective-permute-start.4 = (f32[8,128,128]{2,1,0:T(8,128)S(1)}, f32[8,128,128]{2,1,0:T(8,128)S(1)}, u32[]{:S(2)}, u32[]{:S(2)}) collective-permute-start(f32[8,128,128]{2,1,0:T(8,128)S(1)} %add.641), channel_id=1, source_target_pairs={{0,16},{16,32},{32,48},{48,64},{64,80},{80,96},{96,112},{112,128},... | collective-permute-start | bytes 1572872 | tf_op jit(solution)/shard_map/while/body/eval_jaxpr/ppermute | solution.py:33
  724.1 11.7 %collective-permute-start.4 = (f32[8,128,128]{2,1,0:T(8,128)S(1)}, f32[8,128,128]{2,1,0:T(8,128)S(1)}, u32[]{:S(2)}, u32[]{:S(2)}) collective-permute-start(f32[8,128,128]{2,1,0:T(8,128)S(1)} %add.641), channel_id=1, source_target_pairs={{0,16},{16,32},{32,48},{48,64},{64,80},{80,96},{96,112},{112,128},... | collective-permute-start | bytes 1572872 | tf_op jit(solution)/shard_map/while/body/eval_jaxpr/ppermute | solution.py:33
  743.2 11.7 %collective-permute-start.4 = (f32[8,128,128]{2,1,0:T(8,128)S(1)}, f32[8,128,128]{2,1,0:T(8,128)S(1)}, u32[]{:S(2)}, u32[]{:S(2)}) collective-permute-start(f32[8,128,128]{2,1,0:T(8,128)S(1)} %add.641), channel_id=1, source_target_pairs={{0,16},{16,32},{32,48},{48,64},{64,80},{80,96},{96,112},{112,128},... | collective-permute-start | bytes 1572872 | tf_op jit(solution)/shard_map/while/body/eval_jaxpr/ppermute | solution.py:33
  762.2 11.7 %collective-permute-start.4 = (f32[8,128,128]{2,1,0:T(8,128)S(1)}, f32[8,128,128]{2,1,0:T(8,128)S(1)}, u32[]{:S(2)}, u32[]{:S(2)}) collective-permute-start(f32[8,128,128]{2,1,0:T(8,128)S(1)} %add.641), channel_id=1, source_target_pairs={{0,16},{16,32},{32,48},{48,64},{64,80},{80,96},{96,112},{112,128},... | collective-permute-start | bytes 1572872 | tf_op jit(solution)/shard_map/while/body/eval_jaxpr/ppermute | solution.py:33
  781.3 11.7 %collective-permute-start.4 = (f32[8,128,128]{2,1,0:T(8,128)S(1)}, f32[8,128,128]{2,1,0:T(8,128)S(1)}, u32[]{:S(2)}, u32[]{:S(2)}) collective-permute-start(f32[8,128,128]{2,1,0:T(8,128)S(1)} %add.641), channel_id=1, source_target_pairs={{0,16},{16,32},{32,48},{48,64},{64,80},{80,96},{96,112},{112,128},... | collective-permute-start | bytes 1572872 | tf_op jit(solution)/shard_map/while/body/eval_jaxpr/ppermute | solution.py:33
  800.3 11.7 %collective-permute-start.4 = (f32[8,128,128]{2,1,0:T(8,128)S(1)}, f32[8,128,128]{2,1,0:T(8,128)S(1)}, u32[]{:S(2)}, u32[]{:S(2)}) collective-permute-start(f32[8,128,128]{2,1,0:T(8,128)S(1)} %add.641), channel_id=1, source_target_pairs={{0,16},{16,32},{32,48},{48,64},{64,80},{80,96},{96,112},{112,128},... | collective-permute-start | bytes 1572872 | tf_op jit(solution)/shard_map/while/body/eval_jaxpr/ppermute | solution.py:33
  819.4 11.7 %collective-permute-start.4 = (f32[8,128,128]{2,1,0:T(8,128)S(1)}, f32[8,128,128]{2,1,0:T(8,128)S(1)}, u32[]{:S(2)}, u32[]{:S(2)}) collective-permute-start(f32[8,128,128]{2,1,0:T(8,128)S(1)} %add.641), channel_id=1, source_target_pairs={{0,16},{16,32},{32,48},{48,64},{64,80},{80,96},{96,112},{112,128},... | collective-permute-start | bytes 1572872 | tf_op jit(solution)/shard_map/while/body/eval_jaxpr/ppermute | solution.py:33
  838.4 11.7 %collective-permute-start.4 = (f32[8,128,128]{2,1,0:T(8,128)S(1)}, f32[8,128,128]{2,1,0:T(8,128)S(1)}, u32[]{:S(2)}, u32[]{:S(2)}) collective-permute-start(f32[8,128,128]{2,1,0:T(8,128)S(1)} %add.641), channel_id=1, source_target_pairs={{0,16},{16,32},{32,48},{48,64},{64,80},{80,96},{96,112},{112,128},... | collective-permute-start | bytes 1572872 | tf_op jit(solution)/shard_map/while/body/eval_jaxpr/ppermute | solution.py:33
  857.5 11.7 %collective-permute-start.4 = (f32[8,128,128]{2,1,0:T(8,128)S(1)}, f32[8,128,128]{2,1,0:T(8,128)S(1)}, u32[]{:S(2)}, u32[]{:S(2)}) collective-permute-start(f32[8,128,128]{2,1,0:T(8,128)S(1)} %add.641), channel_id=1, source_target_pairs={{0,16},{16,32},{32,48},{48,64},{64,80},{80,96},{96,112},{112,128},... | collective-permute-start | bytes 1572872 | tf_op jit(solution)/shard_map/while/body/eval_jaxpr/ppermute | solution.py:33
  876.5 11.7 %collective-permute-start.4 = (f32[8,128,128]{2,1,0:T(8,128)S(1)}, f32[8,128,128]{2,1,0:T(8,128)S(1)}, u32[]{:S(2)}, u32[]{:S(2)}) collective-permute-start(f32[8,128,128]{2,1,0:T(8,128)S(1)} %add.641), channel_id=1, source_target_pairs={{0,16},{16,32},{32,48},{48,64},{64,80},{80,96},{96,112},{112,128},... | collective-permute-start | bytes 1572872 | tf_op jit(solution)/shard_map/while/body/eval_jaxpr/ppermute | solution.py:33
  (2 other events, 2.3 us)
where the time goes:
time: 901 us; the launch traced here: 896 us
  waiting for transfers between devices  294 us (33%)
  loops' own time  176 us (20%)
  starting transfers between devices  146 us (16%)
  local copies, waits for them, and re-layouts  145 us (16%)
  other arithmetic  135 us (15%)
    ppermute x30, waiting for transfers between devices, shifted(): return lax.ppermute(block, axis, route)  293 us
    another operation x48, loops' own time, coarse(): return lax.fori_loop(0, sweeps, sweep, source)  163 us
    slice x416, local copies, waits for them, and re-layouts, planar_sum(): jnp.roll(field, -1, 2)  105 us
    ppermute x16, starting transfers between devices, extended_2(): lax.ppermute(head, axis, [((i + 1) % count, i) for i in range(count)])  85 us
    div x192, other arithmetic, sweep(): return (source + weight * planar_sum(guess)) / divisor  80.8 us
    ppermute x30, starting transfers between devices, shifted(): return lax.ppermute(block, axis, route)  57.6 us
    select_n x16, other arithmetic, advance(): return jnp.where(active, moved, center)  41.1 us
    while x61, local copies, waits for them, and re-layouts  18.3 us
  transfers between devices with their start and end apart: 62, of which 39 were waited for; matrix products, arithmetic and copies ran while one was open for 3% of the time, Pallas kernels for 0%

commit v1 on v0

v1 whole, which is shorter than its diff:
```python
import functools

import jax
import jax.numpy as jnp
from jax import lax
from jax.experimental import pallas as pl
from jax.experimental.pallas import tpu as pltpu
from jax.sharding import PartitionSpec as P

FSTEPS = 8
SLICE_TIME = 0.6
MOBILITY = 0.5
WEIGHT = SLICE_TIME * MOBILITY
DIVISOR = 1.0 + 4.0 * WEIGHT
LOWEST_SWEEPS = 2
SWEEPS = 4
MESH = pl.DeviceIdType.MESH


def planar_sum(w):
    last = w.shape[0] - 1
    above = jnp.concatenate([w[1:], pltpu.roll(w[:1], 7, 1)], axis=0)
    below = jnp.concatenate([pltpu.roll(w[last:], 1, 1), w[:last]], axis=0)
    lanes = w.shape[2]
    return (above + below) + (pltpu.roll(w, 1, 2) + pltpu.roll(w, lanes - 1, 2))


def kernel(slices, slabs, init_ref, fine_ref, sweep_ref, out_ref,
           field, entry, given, kept, level_coef, sweep_coef,
           halo_send, halo_recv, chain_send, chain_recv):
    pos = lax.axis_index("tm")
    slab = lax.axis_index("space")
    depth = init_ref.shape[0]
    rows = field.shape[2]
    first, last = pos == 0, pos == slices - 1
    up = lax.rem(slab + 1, slabs)
    down = lax.rem(slab + slabs - 1, slabs)

    barrier = pltpu.get_barrier_semaphore()
    after, before = lax.rem(pos + 1, slices), lax.rem(pos + slices - 1, slices)
    for peer in ({"space": up}, {"space": down}, {"tm": after}, {"tm": before}):
        pl.semaphore_signal(barrier, inc=1, device_id=peer, device_id_type=MESH)

    def halo(turn, side, p):
        return pltpu.make_async_remote_copy(
            src_ref=field.at[turn, depth + p],
            dst_ref=field.at[turn, p + side * 2 * depth],
            send_sem=halo_send.at[turn, side, p],
            recv_sem=halo_recv.at[turn, side, p],
            device_id={"space": down if side else up},
            device_id_type=MESH,
        )

    def chain(turn, p):
        return pltpu.make_async_remote_copy(
            src_ref=given.at[turn, p],
            dst_ref=entry.at[p] if turn else field.at[1, depth + p],
            send_sem=chain_send.at[turn, p],
            recv_sem=chain_recv.at[turn, p],
            device_id={"tm": after},
            device_id_type=MESH,
        )

    tile = level_coef.shape[2:]
    count = jnp.full(tile, fine_ref[0], jnp.int32)
    step = SLICE_TIME / count.astype(jnp.float32)
    for level in range(1, FSTEPS + 1):
        h = jnp.where(count >= level, step, 0.0)
        level_coef[level, 0] = 1.0 - 2.0 * h
        level_coef[level, 1] = h
        level_coef[level, 2] = MOBILITY * h
    sweeps = jnp.full(tile, sweep_ref[0], jnp.int32)
    for turn in range(SWEEPS - LOWEST_SWEEPS):
        active = sweeps >= SWEEPS - turn
        sweep_coef[turn, 0] = jnp.where(active, 1.0 / DIVISOR, 1.0)
        sweep_coef[turn, 1] = jnp.where(active, WEIGHT / DIVISOR, 0.0)

    def coarse(v):
        source = v * ((1.0 + SLICE_TIME) - SLICE_TIME * (v * v))
        w = source
        for turn in range(SWEEPS - LOWEST_SWEEPS):
            w = sweep_coef[turn, 0] * source + sweep_coef[turn, 1] * planar_sum(w)
        source = source * (1.0 / DIVISOR)
        for turn in range(LOWEST_SWEEPS):
            w = source + (WEIGHT / DIVISOR) * planar_sum(w)
        return w

    def load(p, carry):
        for j in range(rows):
            field[0, depth + p, j] = init_ref[p, pl.ds(j, 8, stride=rows), :]

        @pl.when(first)
        def _():
            field[1, depth + p] = field[0, depth + p]
            entry[p] = field[0, depth + p]

        return carry

    lax.fori_loop(0, depth, load, 0)

    def start(n, carry):
        def plane(p, carry):
            field[0, depth + 2 * p] = coarse(field[0, depth + 2 * p])
            field[0, depth + 2 * p + 1] = coarse(field[0, depth + 2 * p + 1])
            return carry

        return lax.fori_loop(0, depth // 2, plane, carry)

    lax.fori_loop(0, pos, start, 0)

    pl.semaphore_wait(barrier, 4)

    def greet(i, carry):
        halo(0, 0, depth - 1 - i).start()
        halo(0, 1, i).start()
        return carry

    lax.fori_loop(0, depth, greet, 0)

    def keep(p, carry):
        kept[p] = coarse(field[0, depth + p])
        return carry

    lax.fori_loop(0, depth, keep, 0)

    def fine(turn, level, z):
        past = ((level + 6) // FSTEPS) * (2 - turn + (level + 1) % 2) + turn
        v = field[past, z]
        side = field[past, z - 1] + field[past, z + 1]
        r = planar_sum(v) + side
        field[2 + level % 2, z] = (
            v * (level_coef[level, 0] - level_coef[level, 1] * (v * v)) + level_coef[level, 2] * r
        )

    half = depth // 2

    def diagonal(turn, d, top):
        def both(level, carry):
            fine(turn, level, depth - d + level)
            fine(turn, level, 2 * depth - 1 + d - level)
            return carry

        lax.fori_loop(1, top + 1, both, 0)

    def relay(turn, p, announce):
        @pl.when(pos > 0)
        def _():
            chain(turn, p).wait_recv()

        if turn == 0:
            announce()
            v = field[1, depth + p]
        else:
            v = entry[p]
        g = coarse(v)
        ended = g + (field[2, depth + p] - kept[p])
        if turn == 0:
            kept[p] = g
        given[turn, p] = ended

        @pl.when(pos < slices - 1)
        def _():
            chain(turn, p).start()

        if turn == 1:
            for j in range(rows):
                out_ref[0, p, pl.ds(j, 8, stride=rows), :] = given[1, p, j]

    for turn in range(2):

        def early(i, carry):
            diagonal(turn, i + 2 - half, i + 1)
            return carry

        lax.fori_loop(0, half - 1, early, 0)

        def wait_halo(d):
            halo(turn, 0, depth - d).wait_recv()
            halo(turn, 1, d - 1).wait_recv()

        def growing(d, carry):
            wait_halo(d)
            diagonal(turn, d, d + half - 1)
            return carry

        lax.fori_loop(1, half + 1, growing, 0)

        def late(d, carry):
            wait_halo(d)
            diagonal(turn, d, FSTEPS)
            lower, upper = depth - d, d - 1

            def tell_lower():
                halo(1, 1, lower).start()

                @pl.when(d == half + 1)
                def _():
                    halo(1, 0, lower).start()

            def tell_upper():
                halo(1, 0, upper).start()

                @pl.when(d == half + 1)
                def _():
                    halo(1, 1, upper).start()

            relay(turn, lower, tell_lower)
            relay(turn, upper, tell_upper)
            return carry

        lax.fori_loop(half + 1, depth + 1, late, 0)

        if turn == 0:

            def rest(i, carry):
                halo(1, 0, half - 2 - i).start()
                halo(1, 1, half + 1 + i).start()
                return carry

            lax.fori_loop(0, half - 1, rest, 0)

    def finish(p, carry):
        for turn in range(2):
            for side in range(2):
                halo(turn, side, p).wait_send()

            @pl.when(pos < slices - 1)
            def _():
                chain(turn, p).wait_send()

        return carry

    lax.fori_loop(0, depth, finish, 0)


def local(initial_state, fine_steps, sweep_count):
    slices, slabs = lax.axis_size("tm"), lax.axis_size("space")
    depth, height, width = initial_state.shape
    plane = (height // 8, 8, width)
    return pl.pallas_call(
        functools.partial(kernel, slices, slabs),
        out_shape=jax.ShapeDtypeStruct((1, *initial_state.shape), jnp.float32),
        in_specs=[
            pl.BlockSpec(memory_space=pltpu.VMEM),
            pl.BlockSpec(memory_space=pltpu.SMEM),
            pl.BlockSpec(memory_space=pltpu.SMEM),
        ],
        out_specs=pl.BlockSpec(memory_space=pltpu.VMEM),
        scratch_shapes=[
            pltpu.VMEM((4, 3 * depth, *plane), jnp.float32),
            pltpu.VMEM((depth, *plane), jnp.float32),
            pltpu.VMEM((2, depth, *plane), jnp.float32),
            pltpu.VMEM((depth, *plane), jnp.float32),
            pltpu.VMEM((FSTEPS + 1, 3, *plane[1:]), jnp.float32),
            pltpu.VMEM((SWEEPS - LOWEST_SWEEPS, 2, *plane[1:]), jnp.float32),
            pltpu.SemaphoreType.DMA((2, 2, depth)),
            pltpu.SemaphoreType.DMA((2, 2, depth)),
            pltpu.SemaphoreType.DMA((2, depth)),
            pltpu.SemaphoreType.DMA((2, depth)),
        ],
        compiler_params=pltpu.CompilerParams(
            collective_id=0, has_side_effects=True, vmem_limit_bytes=48 * 1024 * 1024
        ),
    )(initial_state, fine_steps, sweep_count)


def solution(mesh):
    placed = (P("space", None, None), P("tm"), P())
    return jax.shard_map(
        local, mesh=mesh, in_specs=placed, out_specs=P("tm", "space", None, None), check_vma=False
    )
```

time: 901 us -> 83.5 us (0.09)
  the two profiles are of different devices: /device:TPU:128 before, /device:TPU:225 now
where the time goes in v1:
time: 83.5 us; the launch traced here: 83.4 us
  Pallas kernels  80.2 us (96%)
  local copies, waits for them, and re-layouts  1.83 us (2%)
  between operations  1.31 us (2%)
    pallas_call x1, Pallas kernels, local(): pl.pallas_call(functools.partial(kernel, slices, slabs), out_shape=jax.Sh...  80.2 us
    unnamed x3, local copies, waits for them, and re-layouts  1.83 us

profile of v1, /device:TPU:225, one launch (start us, length us, event | category | flops | bytes accessed | tf_op | source)
XLA Modules:
  0.0 83.4 jit_solution(9318250119649619017)
XLA Ops:
  1.3 0.0 copy-start
  1.3 1.0 %copy-done = f32[8,128,128]{2,1,0:T(8,128)S(1)} copy-done((f32[8,128,128]{2,1,0:T(8,128)S(1)}, f32[8,128,128]{2,1,0:T(8,128)}, u32[]{:S(2)}) %copy-start) | copy-done | bytes 524312
  2.3 80.2 %shard_map.37 = f32[1,8,128,128]{3,2,1,0:T(8,128)S(1)} custom-call(f32[8,128,128]{2,1,0:T(8,128)S(1)} %copy-done, s32[1]{0:T(128)S(6)} %copy.5.fine_ref, s32[1]{0:T(128)S(6)} %copy.6.sweep_ref), custom_call_target="tpu_custom_call" | custom-call | tf_op jit(solution)/shard_map/pallas_call | solution.py:240
  82.6 0.8 copy.7
Async XLA Ops:
  1.3 1.0 %copy-start = (f32[8,128,128]{2,1,0:T(8,128)S(1)}, f32[8,128,128]{2,1,0:T(8,128)}, u32[]{:S(2)}) copy-start(f32[8,128,128]{2,1,0:T(8,128)} %init_ref.1) | copy-start | bytes 1572868

commit v2 on v1

v2 whole, which is shorter than its diff:
```python
import functools

import jax
import jax.numpy as jnp
from jax import lax
from jax.experimental import pallas as pl
from jax.experimental.pallas import tpu as pltpu
from jax.sharding import PartitionSpec as P

FSTEPS = 8
SLICE_TIME = 0.6
MOBILITY = 0.5
WEIGHT = SLICE_TIME * MOBILITY
DIVISOR = 1.0 + 4.0 * WEIGHT
LOWEST_SWEEPS = 2
SWEEPS = 4
MESH = pl.DeviceIdType.MESH


def planar_sum(w):
    lanes = w[0].shape[1]
    above = w[1:] + [pltpu.roll(w[0], 7, 0)]
    below = [pltpu.roll(w[-1], 1, 0)] + w[:-1]
    return [
        (pltpu.roll(w[j], 1, 1) + pltpu.roll(w[j], lanes - 1, 1)) + (above[j] + below[j])
        for j in range(len(w))
    ]


def kernel(slices, slabs, init_ref, fine_ref, sweep_ref, out_ref,
           field, state, solved, kept, final, level_coef, sweep_coef,
           halo_send, halo_recv, chain_send, chain_recv, pair_send, pair_recv):
    pos = lax.axis_index("tm")
    slab = lax.axis_index("space")
    chip, core = pos // 2, pos % 2
    chips = slices // 2
    depth = init_ref.shape[0]
    half = depth // 2
    rows = field.shape[2]

    barrier = pltpu.get_barrier_semaphore()
    peers = (
        {"space": (slab + 1) % slabs},
        {"space": (slab + slabs - 1) % slabs},
        {"tm": pos + 1 - 2 * core},
        {"tm": (pos + 2) % slices},
        {"tm": (pos + slices - 2) % slices},
    )
    for peer in peers:
        pl.semaphore_signal(barrier, inc=1, device_id=peer, device_id_type=MESH)

    def mine(i):
        return half - 1 - i + core * (1 + 2 * i)

    def theirs(i):
        return half + i - core * (1 + 2 * i)

    def halo(turn, side, p):
        return pltpu.make_async_remote_copy(
            src_ref=field.at[turn, depth + p],
            dst_ref=field.at[turn, p + side * (2 * depth)],
            send_sem=halo_send.at[turn, side, p],
            recv_sem=halo_recv.at[turn, side, p],
            device_id={"space": (slab + 1 + side * (slabs - 2)) % slabs},
            device_id_type=MESH,
        )

    def chain(turn, i):
        return pltpu.make_async_remote_copy(
            src_ref=state.at[1 + turn, 2, i],
            dst_ref=state.at[1 + turn, 0, i],
            send_sem=chain_send.at[turn, i],
            recv_sem=chain_recv.at[turn, i],
            device_id={"tm": (pos + 2) % slices},
            device_id_type=MESH,
        )

    def pair(kind, src, dst, i):
        return pltpu.make_async_remote_copy(
            src_ref=src,
            dst_ref=dst,
            send_sem=pair_send.at[kind, i],
            recv_sem=pair_recv.at[kind, i],
            device_id={"tm": pos + 1 - 2 * core},
            device_id_type=MESH,
        )

    def share(turn, i):
        return pair(turn, state.at[turn, 1 - core, i], field.at[turn, depth + mine(i)], i)

    def share_solved(turn, i):
        return pair(2 + turn, field.at[2, depth + theirs(i)], solved.at[turn, core, i], i)

    def share_final(i):
        return pair(4, state.at[2, 2 - core, i], final.at[i], i)

    tile = level_coef.shape[2:]
    count = jnp.full(tile, fine_ref[0], jnp.int32)
    step = SLICE_TIME / count.astype(jnp.float32)
    for level in range(1, FSTEPS + 1):
        h = jnp.where(count >= level, step, 0.0)
        level_coef[level, 0] = 1.0 - 2.0 * h
        level_coef[level, 1] = h
        level_coef[level, 2] = MOBILITY * h
    sweeps = jnp.full(tile, sweep_ref[0], jnp.int32)
    for power in range(SWEEPS + 1):
        factor = (WEIGHT / DIVISOR) ** power
        inner = jnp.where(sweeps > power, factor / DIVISOR, 0.0)
        sweep_coef[power] = jnp.where(sweeps == power, factor, inner)

    def get(ref, *at):
        return [ref[(*at, j)] for j in range(rows)]

    def put(ref, values, *at):
        for j in range(rows):
            ref[(*at, j)] = values[j]

    def coarse(v):
        power = [x * ((1.0 + SLICE_TIME) - SLICE_TIME * (x * x)) for x in v]
        total = [sweep_coef[0] * x for x in power]
        for turn in range(SWEEPS):
            power = planar_sum(power)
            total = [t + sweep_coef[turn + 1] * x for t, x in zip(total, power)]
        return total

    def load(i, carry):
        for j in range(rows):
            state[0, 0, i, j] = init_ref[mine(i), pl.ds(j, 8, stride=rows), :]

        @pl.when(chip == 0)
        def _():
            state[1, 0, i] = state[0, 0, i]
            state[2, 0, i] = state[0, 0, i]

        return carry

    lax.fori_loop(0, half, load, 0)

    def start(n, carry):
        def plane(i, carry):
            put(state, coarse(get(state, 0, 0, i)), 0, 0, i)
            return carry

        return lax.fori_loop(0, half, plane, carry)

    lax.fori_loop(0, 2 * chip, start, 0)
    pl.semaphore_wait(barrier, len(peers))

    def deal(t, carry):
        i = half - 1 - t
        g = coarse(get(state, 0, 0, i))
        put(state, g, 0, 1, i)
        share(0, i).start()
        put(kept, g, 0, i)
        put(field, get(state, 0, core, i), 0, depth + mine(i))
        halo(0, 1 - core, mine(i)).start()
        return carry

    lax.fori_loop(0, half, deal, 0)

    def greet(t, carry):
        i = half - 1 - t
        share(0, i).wait_recv()
        halo(0, core, theirs(i)).start()
        return carry

    lax.fori_loop(0, half, greet, 0)

    def rest(turn):
        def body(i, carry):
            halo(turn, 0, half - 1 - i).start()
            halo(turn, 1, half + i).start()
            return carry

        lax.fori_loop(0, half, body, 0)

    rest(0)

    def keep(i, carry):
        put(kept, coarse(get(state, 0, 1, i)), 1, i)
        return carry

    lax.fori_loop(0, half, keep, 0)

    def fine(turn, level, z):
        past = ((level + 6) // FSTEPS) * (2 - turn + (level + 1) % 2) + turn
        v = get(field, past, z)
        r = planar_sum(v)
        a, h, b = level_coef[level, 0], level_coef[level, 1], level_coef[level, 2]
        for j in range(rows):
            around = r[j] + (field[past, z - 1, j] + field[past, z + 1, j])
            field[2 + level % 2, z, j] = v[j] * (a - h * (v[j] * v[j])) + b * around

    def diagonal(turn, d, top):
        def both(level, carry):
            fine(turn, level, depth - d + level)
            fine(turn, level, 2 * depth - 1 + d - level)
            return carry

        lax.fori_loop(1, top + 1, both, 0)

    def wait_halo(turn, d):
        halo(turn, 0, depth - d).wait_recv()
        halo(turn, 1, d - 1).wait_recv()

    def finish(turn, i):
        wait_halo(turn, half + 1 + i)
        diagonal(turn, half + 1 + i, FSTEPS)
        share_solved(turn, i).start()
        put(solved, get(field, 2, depth + mine(i)), turn, core, i)

    def relay(turn, i):
        @pl.when(chip > 0)
        def _():
            chain(turn, i).wait_recv()

        g = coarse(get(state, 1 + turn, 0, i))
        share_solved(turn, i).wait_recv()
        for j in range(rows):
            state[1 + turn, 1, i, j] = g[j] + (solved[turn, 0, i, j] - kept[0, i, j])
        if turn == 0:
            put(kept, g, 0, i)
            share(1, i).start()
        g = coarse(get(state, 1 + turn, 1, i))
        for j in range(rows):
            state[1 + turn, 2, i, j] = g[j] + (solved[turn, 1, i, j] - kept[1, i, j])

        @pl.when(chip < chips - 1)
        def _():
            chain(turn, i).start()

        if turn == 0:
            put(kept, g, 1, i)
            put(field, get(state, 1, core, i), 1, depth + mine(i))
            halo(1, 1 - core, mine(i)).start()
        else:
            share_final(i).start()
            for j in range(rows):
                out_ref[0, mine(i), pl.ds(j, 8, stride=rows), :] = state[2, 1 + core, i, j]

    def tell(i):
        share(1, i).wait_recv()
        halo(1, core, theirs(i)).start()

    for turn in range(2):

        def early(i, carry):
            diagonal(turn, i + 2 - half, i + 1)
            return carry

        lax.fori_loop(0, half - 1, early, 0)

        def growing(d, carry):
            wait_halo(turn, d)
            diagonal(turn, d, d + half - 1)
            return carry

        lax.fori_loop(1, half + 1, growing, 0)
        finish(turn, 0)

        def late(i, carry):
            finish(turn, i)
            relay(turn, i - 1)
            if turn == 0:

                @pl.when(i > 1)
                def _():
                    tell(i - 2)

            return carry

        lax.fori_loop(1, half, late, 0)
        if turn == 0:
            tell(half - 2)
        relay(turn, half - 1)
        if turn == 0:
            tell(half - 1)
            rest(1)

            def sent(i, carry):
                share_solved(0, i).wait_send()
                return carry

            lax.fori_loop(0, half, sent, 0)

    def gather(i, carry):
        share_final(i).wait_recv()
        for j in range(rows):
            out_ref[0, theirs(i), pl.ds(j, 8, stride=rows), :] = final[i, j]
        return carry

    lax.fori_loop(0, half, gather, 0)

    def drain(i, carry):
        for turn in range(2):
            for side in range(2):
                halo(turn, side, i).wait_send()
                halo(turn, side, half + i).wait_send()

            @pl.when(chip < chips - 1)
            def _():
                chain(turn, i).wait_send()

            share(turn, i).wait_send()
        share_solved(1, i).wait_send()
        share_final(i).wait_send()
        return carry

    lax.fori_loop(0, half, drain, 0)


def local(initial_state, fine_steps, sweep_count):
    slices, slabs = lax.axis_size("tm"), lax.axis_size("space")
    depth, height, width = initial_state.shape
    plane = (height // 8, 8, width)
    half = depth // 2
    return pl.pallas_call(
        functools.partial(kernel, slices, slabs),
        out_shape=jax.ShapeDtypeStruct((1, *initial_state.shape), jnp.float32),
        in_specs=[
            pl.BlockSpec(memory_space=pltpu.VMEM),
            pl.BlockSpec(memory_space=pltpu.SMEM),
            pl.BlockSpec(memory_space=pltpu.SMEM),
        ],
        out_specs=pl.BlockSpec(memory_space=pltpu.VMEM),
        scratch_shapes=[
            pltpu.VMEM((4, 3 * depth, *plane), jnp.float32),
            pltpu.VMEM((3, 3, half, *plane), jnp.float32),
            pltpu.VMEM((2, 2, half, *plane), jnp.float32),
            pltpu.VMEM((2, half, *plane), jnp.float32),
            pltpu.VMEM((half, *plane), jnp.float32),
            pltpu.VMEM((FSTEPS + 1, 3, *plane[1:]), jnp.float32),
            pltpu.VMEM((SWEEPS + 1, *plane[1:]), jnp.float32),
            pltpu.SemaphoreType.DMA((2, 2, depth)),
            pltpu.SemaphoreType.DMA((2, 2, depth)),
            pltpu.SemaphoreType.DMA((2, half)),
            pltpu.SemaphoreType.DMA((2, half)),
            pltpu.SemaphoreType.DMA((5, half)),
            pltpu.SemaphoreType.DMA((5, half)),
        ],
        compiler_params=pltpu.CompilerParams(
            collective_id=0, has_side_effects=True, vmem_limit_bytes=48 * 1024 * 1024
        ),
    )(initial_state, fine_steps, sweep_count)


def solution(mesh):
    placed = (P("space", None, None), P("tm"), P())
    return jax.shard_map(
        local, mesh=mesh, in_specs=placed, out_specs=P("tm", "space", None, None), check_vma=False
    )
```

time: 83.5 us -> 96.3 us (1.15)
  Pallas kernels: 80.2 us -> 92.8 us
    pallas_call x1, Pallas kernels: 80.2 us -> 92.8 us  [local(): pl.pallas_call(functools.partial(kernel, slices, slabs), out_shape=jax.Sh...]
where the time goes in v2:
time: 96.3 us; the launch traced here: 95.9 us
  Pallas kernels  92.8 us (96%)
  local copies, waits for them, and re-layouts  1.83 us (2%)
  between operations  1.31 us (1%)
    pallas_call x1, Pallas kernels, local(): pl.pallas_call(functools.partial(kernel, slices, slabs), out_shape=jax.Sh...  92.8 us

profile of v2, /device:TPU:225, one launch (start us, length us, event | category | flops | bytes accessed | tf_op | source)
XLA Modules:
  0.0 95.9 jit_solution(10436945827956370687)
XLA Ops:
  1.3 0.0 copy-start
  1.3 1.0 %copy-done = f32[8,128,128]{2,1,0:T(8,128)S(1)} copy-done((f32[8,128,128]{2,1,0:T(8,128)S(1)}, f32[8,128,128]{2,1,0:T(8,128)}, u32[]{:S(2)}) %copy-start) | copy-done | bytes 524312
  2.3 92.8 %shard_map.37 = f32[1,8,128,128]{3,2,1,0:T(8,128)S(1)} custom-call(f32[8,128,128]{2,1,0:T(8,128)S(1)} %copy-done, s32[1]{0:T(128)S(6)} %copy.5.fine_ref, s32[1]{0:T(128)S(6)} %copy.6.sweep_ref), custom_call_target="tpu_custom_call" | custom-call | tf_op jit(solution)/shard_map/pallas_call | solution.py:317
  95.1 0.8 copy.7
Async XLA Ops:
  1.3 1.0 %copy-start = (f32[8,128,128]{2,1,0:T(8,128)S(1)}, f32[8,128,128]{2,1,0:T(8,128)}, u32[]{:S(2)}) copy-start(f32[8,128,128]{2,1,0:T(8,128)} %init_ref.1) | copy-start | bytes 1572868

commit v3 on v2

--- a/solution.py
+++ b/solution.py
@@ -187,14 +187,15 @@
         v = get(field, past, z)
         r = planar_sum(v)
         a, h, b = level_coef[level, 0], level_coef[level, 1], level_coef[level, 2]
-        for j in range(rows):
-            around = r[j] + (field[past, z - 1, j] + field[past, z + 1, j])
-            field[2 + level % 2, z, j] = v[j] * (a - h * (v[j] * v[j])) + b * around
+        r = [x + (y + z) for x, y, z in zip(r, get(field, past, z - 1), get(field, past, z + 1))]
+        return [x * (a - h * (x * x)) + b * y for x, y in zip(v, r)]
 
     def diagonal(turn, d, top):
         def both(level, carry):
-            fine(turn, level, depth - d + level)
-            fine(turn, level, 2 * depth - 1 + d - level)
+            low, high = depth - d + level, 2 * depth - 1 + d - level
+            below, above = fine(turn, level, low), fine(turn, level, high)
+            put(field, below, 2 + level % 2, low)
+            put(field, above, 2 + level % 2, high)
             return carry
 
         lax.fori_loop(1, top + 1, both, 0)
@@ -216,14 +217,14 @@
 
         g = coarse(get(state, 1 + turn, 0, i))
         share_solved(turn, i).wait_recv()
-        for j in range(rows):
-            state[1 + turn, 1, i, j] = g[j] + (solved[turn, 0, i, j] - kept[0, i, j])
+        jump = zip(g, get(solved, turn, 0, i), get(kept, 0, i))
+        put(state, [x + (y - z) for x, y, z in jump], 1 + turn, 1, i)
         if turn == 0:
             put(kept, g, 0, i)
             share(1, i).start()
         g = coarse(get(state, 1 + turn, 1, i))
-        for j in range(rows):
-            state[1 + turn, 2, i, j] = g[j] + (solved[turn, 1, i, j] - kept[1, i, j])
+        jump = zip(g, get(solved, turn, 1, i), get(kept, 1, i))
+        put(state, [x + (y - z) for x, y, z in jump], 1 + turn, 2, i)
 
         @pl.when(chip < chips - 1)
         def _():

time: 96.3 us -> 76.2 us (0.79)
  Pallas kernels: 92.8 us -> 73 us
    pallas_call x1, Pallas kernels: 92.8 us -> 73 us  [local(): pl.pallas_call(functools.partial(kernel, slices, slabs), out_shape=jax.Sh...]
where the time goes in v3:
time: 76.2 us; the launch traced here: 76.1 us
  Pallas kernels  73 us (96%)
  local copies, waits for them, and re-layouts  1.83 us (2%)
  between operations  1.31 us (2%)
    pallas_call x1, Pallas kernels, local(): pl.pallas_call(functools.partial(kernel, slices, slabs), out_shape=jax.Sh...  73 us
    unnamed x3, local copies, waits for them, and re-layouts  1.83 us

profile of v3, /device:TPU:225, one launch (start us, length us, event | category | flops | bytes accessed | tf_op | source)
XLA Modules:
  0.0 76.1 jit_solution(2164571401549494433)
XLA Ops:
  1.3 0.0 copy-start
  1.3 1.0 %copy-done = f32[8,128,128]{2,1,0:T(8,128)S(1)} copy-done((f32[8,128,128]{2,1,0:T(8,128)S(1)}, f32[8,128,128]{2,1,0:T(8,128)}, u32[]{:S(2)}) %copy-start) | copy-done | bytes 524312
  2.3 73.0 %shard_map.37 = f32[1,8,128,128]{3,2,1,0:T(8,128)S(1)} custom-call(f32[8,128,128]{2,1,0:T(8,128)S(1)} %copy-done, s32[1]{0:T(128)S(6)} %copy.5.fine_ref, s32[1]{0:T(128)S(6)} %copy.6.sweep_ref), custom_call_target="tpu_custom_call" | custom-call | tf_op jit(solution)/shard_map/pallas_call | solution.py:318
  75.3 0.8 %copy.7 = f32[1,8,128,128]{3,2,1,0:T(8,128)} copy(f32[1,8,128,128]{3,2,1,0:T(8,128)S(1)} %shard_map.37) | data formatting | bytes 1048576
Async XLA Ops:
  1.3 1.0 %copy-start = (f32[8,128,128]{2,1,0:T(8,128)S(1)}, f32[8,128,128]{2,1,0:T(8,128)}, u32[]{:S(2)}) copy-start(f32[8,128,128]{2,1,0:T(8,128)} %init_ref.1) | copy-start | bytes 1572868

commit v4 on v2

v4 whole, which is shorter than its diff:
```python
import functools

import jax
import jax.numpy as jnp
from jax import lax
from jax.experimental import pallas as pl
from jax.experimental.pallas import tpu as pltpu
from jax.sharding import PartitionSpec as P

FSTEPS = 8
SLICE_TIME = 0.6
MOBILITY = 0.5
WEIGHT = SLICE_TIME * MOBILITY
DIVISOR = 1.0 + 4.0 * WEIGHT
LOWEST_SWEEPS = 2
SWEEPS = 4
MESH = pl.DeviceIdType.MESH


def planar_sum(w):
    last, lanes = w.shape[0] - 1, w.shape[2]
    above = jnp.concatenate([w[1:], pltpu.roll(w[:1], 7, 1)], axis=0)
    below = jnp.concatenate([pltpu.roll(w[last:], 1, 1), w[:last]], axis=0)
    return (above + below) + (pltpu.roll(w, 1, 2) + pltpu.roll(w, lanes - 1, 2))


def kernel(slices, slabs, init_ref, fine_ref, sweep_ref, out_ref,
           fetched, level0, odd, even, intake_planes, state, solved, kept, final, level_coef, sweep_coef, fetch_sem,
           halo_send, halo_recv, chain_send, chain_recv, pair_send, pair_recv,
           side_send, side_recv):
    pos = lax.axis_index("tm")
    slab = lax.axis_index("space")
    chip, core = pos // 2, pos % 2
    chips = slices // 2
    depth = init_ref.shape[0]
    half = depth // 2
    rows = even.shape[1]
    other = pos + 1 - 2 * core

    barrier = pltpu.get_barrier_semaphore()
    above, below = (slab + 1) % slabs, (slab + slabs - 1) % slabs
    peers = (
        {"space": above},
        {"space": below},
        {"space": above, "tm": other},
        {"space": below, "tm": other},
        {"tm": other},
        {"tm": (pos + 2) % slices},
        {"tm": (pos + slices - 2) % slices},
    )
    for peer in peers:
        pl.semaphore_signal(barrier, inc=1, device_id=peer, device_id_type=MESH)

    fetch = pltpu.make_async_copy(init_ref.at[pl.ds(half * core, half)], fetched, fetch_sem)
    fetch.start()

    def mine(i):
        return half - 1 - i + core * (1 + 2 * i)

    def theirs(i):
        return half + i - core * (1 + 2 * i)

    def halo(turn, side, piece, i):
        p = mine(i)
        if turn == 0:
            target, core_there = intake_planes.at[depth - 1 - p + side * (2 * p + 1 - depth), 0], side
        else:
            target, core_there = level0.at[1, p + side * (2 * depth)], piece
        return pltpu.make_async_remote_copy(
            src_ref=state.at[turn, piece, i],
            dst_ref=target,
            send_sem=halo_send.at[turn, side, piece, i],
            recv_sem=halo_recv.at[turn, side, p],
            device_id={
                "space": (slab + 1 + side * (slabs - 2)) % slabs,
                "tm": 2 * chip + core_there,
            },
            device_id_type=MESH,
        )

    def wait_side(turn, side, p):
        pltpu.make_async_remote_copy(
            src_ref=state.at[turn, core, 0],
            dst_ref=state.at[turn, core, 0],
            send_sem=halo_send.at[turn, side, 0, 0],
            recv_sem=halo_recv.at[turn, side, p],
            device_id={"space": (slab + 1 + side * (slabs - 2)) % slabs},
            device_id_type=MESH,
        ).wait_recv()

    def share_side(d):
        return pltpu.make_async_remote_copy(
            src_ref=intake_planes.at[d - 1, 1 - core],
            dst_ref=level0.at[0, depth - d + core * (depth + 2 * d - 1)],
            send_sem=side_send.at[d - 1],
            recv_sem=side_recv.at[d - 1],
            device_id={"tm": other},
            device_id_type=MESH,
        )

    def chain(turn, i):
        return pltpu.make_async_remote_copy(
            src_ref=state.at[1 + turn, 2, i],
            dst_ref=state.at[1 + turn, 0, i],
            send_sem=chain_send.at[turn, i],
            recv_sem=chain_recv.at[turn, i],
            device_id={"tm": (pos + 2) % slices},
            device_id_type=MESH,
        )

    def pair(kind, src, dst, i):
        return pltpu.make_async_remote_copy(
            src_ref=src,
            dst_ref=dst,
            send_sem=pair_send.at[kind, i],
            recv_sem=pair_recv.at[kind, i],
            device_id={"tm": other},
            device_id_type=MESH,
        )

    def share(turn, i):
        return pair(turn, state.at[turn, 1 - core, i], level0.at[turn, depth + mine(i)], i)

    def share_solved(turn, i):
        return pair(2 + turn, even.at[depth + theirs(i)], solved.at[turn, core, i], i)

    def share_final(i):
        return pair(4, state.at[2, 2 - core, i], final.at[i], i)

    tile = level_coef.shape[2:]
    count = jnp.full(tile, fine_ref[0], jnp.int32)
    step = SLICE_TIME / count.astype(jnp.float32)
    for level in range(1, FSTEPS + 1):
        h = jnp.where(count >= level, step, 0.0)
        level_coef[level, 0] = 1.0 - 2.0 * h
        level_coef[level, 1] = h
        level_coef[level, 2] = MOBILITY * h
    sweeps = jnp.full(tile, sweep_ref[0], jnp.int32)
    for power in range(SWEEPS + 1):
        factor = (WEIGHT / DIVISOR) ** power
        inner = jnp.where(sweeps > power, factor / DIVISOR, 0.0)
        sweep_coef[power] = jnp.where(sweeps == power, factor, inner)

    def coarse(v):
        power = v * ((1.0 + SLICE_TIME) - SLICE_TIME * (v * v))
        total = sweep_coef[0] * power
        for turn in range(SWEEPS):
            power = planar_sum(power)
            total = total + sweep_coef[turn + 1] * power
        return total

    def load(i, carry):
        for j in range(rows):
            state[0, 0, i, j] = fetched[mine(i) - half * core, pl.ds(j, 8, stride=rows), :]

        @pl.when(chip == 0)
        def _():
            state[1, 0, i] = state[0, 0, i]
            state[2, 0, i] = state[0, 0, i]

        return carry

    fetch.wait()
    lax.fori_loop(0, half, load, 0)

    def start(n, carry):
        def plane(i, carry):
            state[0, 0, i] = coarse(state[0, 0, i])
            return carry

        return lax.fori_loop(0, half, plane, carry)

    lax.fori_loop(0, 2 * chip, start, 0)
    def deal(i, carry):
        g = coarse(state[0, 0, i])
        state[0, 1, i] = g
        kept[0, i] = g
        level0[0, depth + mine(i)] = state[0, core, i]
        kept[1, i] = coarse(g)
        return carry

    lax.fori_loop(0, half, deal, 0)
    pl.semaphore_wait(barrier, len(peers))

    def near(turn, i):
        for piece in range(1 + turn):
            halo(turn, 1 - core, piece, i).start()

    def far(turn):
        def left(t, carry):
            for piece in range(1 + turn):
                halo(turn, 1 - core, piece, 1 - turn + t).wait_send()
            return carry

        lax.fori_loop(0, half - 1, left, 0)

        def go(i, carry):
            for piece in range(1 + turn):
                halo(turn, core, piece, i).start()
            return carry

        lax.fori_loop(0, half, go, 0)

    def greet(t, carry):
        near(0, half - 1 - t)
        share(0, half - 1 - t).start()
        return carry

    lax.fori_loop(0, half, greet, 0)

    def intake(d):
        wait_side(0, core, depth - d + core * (2 * d - 1 - depth))
        intake_planes[d - 1, 1] = coarse(intake_planes[d - 1, 0])
        share_side(d).start()
        level0[0, depth - d + core * (depth + 2 * d - 1)] = intake_planes[d - 1, core]

    def step(past, to, level, d):
        for z in (depth - d + level, 2 * depth - 1 + d - level):
            v = past[z]
            r = planar_sum(v) + (past[z - 1] + past[z + 1])
            a, h, b = level_coef[level, 0], level_coef[level, 1], level_coef[level, 2]
            to[z] = v * (a - h * (v * v)) + b * r

    def diagonal(turn, d, top):
        step(level0.at[turn], odd, 1, d)

        def two(m, carry):
            step(odd, even, 2 * m, d)
            step(even, odd, 2 * m + 1, d)
            return carry

        lax.fori_loop(1, (top + 1) // 2, two, 0)
        if top % 2 == 0:
            step(odd, even, top, d)

    def wait_halo(turn, d):
        if turn == 0:
            share_side(d).wait_recv()
        else:
            wait_side(turn, 0, depth - d)
            wait_side(turn, 1, d - 1)

    def finish(turn, i):
        wait_halo(turn, half + 1 + i)
        diagonal(turn, half + 1 + i, FSTEPS)
        share_solved(turn, i).start()
        solved[turn, core, i] = even[depth + mine(i)]

    def relay(turn, i):
        @pl.when(chip > 0)
        def _():
            chain(turn, i).wait_recv()

        g = coarse(state[1 + turn, 0, i])
        share_solved(turn, i).wait_recv()
        state[1 + turn, 1, i] = g + (solved[turn, 0, i] - kept[0, i])
        if turn == 0:
            kept[0, i] = g
            share(1, i).start()
        g = coarse(state[1 + turn, 1, i])
        state[1 + turn, 2, i] = g + (solved[turn, 1, i] - kept[1, i])

        @pl.when(chip < chips - 1)
        def _():
            chain(turn, i).start()

        if turn == 0:
            kept[1, i] = g
            near(1, i)
            level0[1, depth + mine(i)] = state[1, core, i]
        else:
            share_final(i).start()
            for j in range(rows):
                out_ref[0, mine(i), pl.ds(j, 8, stride=rows), :] = state[2, 1 + core, i, j]

    for turn in range(2):

        def own(i, carry):
            share(turn, i).wait_recv()
            return carry

        lax.fori_loop(0, half, own, 0)
        for d in range(2 - half, 1):
            diagonal(turn, d, half - 1 + d)
        far(turn)
        if turn == 0:
            intake(1)
        for d in range(1, half + 1):
            if turn == 0:
                intake(d + 1)
            wait_halo(turn, d)
            diagonal(turn, d, half - 1 + d)
        if turn == 0:
            intake(half + 2)
        finish(turn, 0)

        def late(i, carry):
            if turn == 0:

                @pl.when(i < half - 1)
                def _():
                    intake(half + 2 + i)

            finish(turn, i)
            relay(turn, i - 1)
            return carry

        lax.fori_loop(1, half, late, 0)
        relay(turn, half - 1)

        def sent(i, carry):
            share_solved(turn, i).wait_send()
            return carry

        lax.fori_loop(0, half, sent, 0)

    def gather(i, carry):
        share_final(i).wait_recv()
        for j in range(rows):
            out_ref[0, theirs(i), pl.ds(j, 8, stride=rows), :] = final[i, j]
        return carry

    lax.fori_loop(0, half, gather, 0)

    def drain(i, carry):
        for turn in range(2):
            share_side(1 + turn * half + i).wait_send()
            for piece in range(1 + turn):
                halo(turn, core, piece, i).wait_send()

                @pl.when(i == (half - 1) * turn)
                def _():
                    halo(turn, 1 - core, piece, i).wait_send()

            @pl.when(chip < chips - 1)
            def _():
                chain(turn, i).wait_send()

            share(turn, i).wait_send()
        share_final(i).wait_send()
        return carry

    lax.fori_loop(0, half, drain, 0)


def local(initial_state, fine_steps, sweep_count):
    slices, slabs = lax.axis_size("tm"), lax.axis_size("space")
    depth, height, width = initial_state.shape
    plane = (height // 8, 8, width)
    half = depth // 2
    return pl.pallas_call(
        functools.partial(kernel, slices, slabs),
        out_shape=jax.ShapeDtypeStruct((1, *initial_state.shape), jnp.float32),
        in_specs=[
            pl.BlockSpec(memory_space=pltpu.HBM),
            pl.BlockSpec(memory_space=pltpu.SMEM),
            pl.BlockSpec(memory_space=pltpu.SMEM),
        ],
        out_specs=pl.BlockSpec(memory_space=pltpu.VMEM),
        scratch_shapes=[
            pltpu.VMEM((half, height, width), jnp.float32),
            pltpu.VMEM((2, 3 * depth, *plane), jnp.float32),
            pltpu.VMEM((3 * depth, *plane), jnp.float32),
            pltpu.VMEM((3 * depth, *plane), jnp.float32),
            pltpu.VMEM((depth, 2, *plane), jnp.float32),
            pltpu.VMEM((3, 3, half, *plane), jnp.float32),
            pltpu.VMEM((2, 2, half, *plane), jnp.float32),
            pltpu.VMEM((2, half, *plane), jnp.float32),
            pltpu.VMEM((half, *plane), jnp.float32),
            pltpu.VMEM((FSTEPS + 1, 3, *plane[1:]), jnp.float32),
            pltpu.VMEM((SWEEPS + 1, *plane[1:]), jnp.float32),
            pltpu.SemaphoreType.DMA,
            pltpu.SemaphoreType.DMA((2, 2, 2, half)),
            pltpu.SemaphoreType.DMA((2, 2, depth)),
            pltpu.SemaphoreType.DMA((2, half)),
            pltpu.SemaphoreType.DMA((2, half)),
            pltpu.SemaphoreType.DMA((5, half)),
            pltpu.SemaphoreType.DMA((5, half)),
            pltpu.SemaphoreType.DMA((depth,)),
            pltpu.SemaphoreType.DMA((depth,)),
        ],
        compiler_params=pltpu.CompilerParams(
            collective_id=0, has_side_effects=True, vmem_limit_bytes=48 * 1024 * 1024
        ),
    )(initial_state, fine_steps, sweep_count)


def solution(mesh):
    placed = (P("space", None, None), P("tm"), P())
    return jax.shard_map(
        local, mesh=mesh, in_specs=placed, out_specs=P("tm", "space", None, None), check_vma=False
    )
```

time: 96.3 us -> 75.5 us (0.78)
  Pallas kernels: 92.8 us -> 71 us
    pallas_call x1, Pallas kernels: 92.8 us -> 71 us  [local(): pl.pallas_call(functools.partial(kernel, slices, slabs), out_shape=jax.Sh...]
where the time goes in v4:
time: 75.5 us; the launch traced here: 74.2 us
  Pallas kernels  71 us (94%)
  local copies, waits for them, and re-layouts  1.83 us (2%)
  between operations  1.31 us (2%)
    pallas_call x1, Pallas kernels, local(): pl.pallas_call(functools.partial(kernel, slices, slabs), out_shape=jax.Sh...  71 us
    unnamed x3, local copies, waits for them, and re-layouts  1.83 us

profile of v4, /device:TPU:225, one launch (start us, length us, event | category | flops | bytes accessed | tf_op | source)
XLA Modules:
  0.0 74.2 jit_solution(13909749213208988067)
XLA Ops:
  1.3 0.0 copy-start
  1.3 1.0 %copy-done = f32[8,128,128]{2,1,0:T(8,128)S(1)} copy-done((f32[8,128,128]{2,1,0:T(8,128)S(1)}, f32[8,128,128]{2,1,0:T(8,128)}, u32[]{:S(2)}) %copy-start) | copy-done | bytes 524312
  2.3 71.0 %shard_map.37 = f32[1,8,128,128]{3,2,1,0:T(8,128)S(1)} custom-call(f32[8,128,128]{2,1,0:T(8,128)S(1)} %copy-done, s32[1]{0:T(128)S(6)} %copy.5.fine_ref, s32[1]{0:T(128)S(6)} %copy.6.sweep_ref), custom_call_target="tpu_custom_call" | custom-call | tf_op jit(solution)/shard_map/pallas_call | solution.py:351
  73.4 0.8 %copy.7 = f32[1,8,128,128]{3,2,1,0:T(8,128)} copy(f32[1,8,128,128]{3,2,1,0:T(8,128)S(1)} %shard_map.37) | data formatting | bytes 1048576
Async XLA Ops:
  1.3 1.0 %copy-start = (f32[8,128,128]{2,1,0:T(8,128)S(1)}, f32[8,128,128]{2,1,0:T(8,128)}, u32[]{:S(2)}) copy-start(f32[8,128,128]{2,1,0:T(8,128)} %init_ref.1) | copy-start | bytes 1572868

commit v5 on v4

--- a/solution.py
+++ b/solution.py
@@ -22,6 +22,16 @@
     above = jnp.concatenate([w[1:], pltpu.roll(w[:1], 7, 1)], axis=0)
     below = jnp.concatenate([pltpu.roll(w[last:], 1, 1), w[:last]], axis=0)
     return (above + below) + (pltpu.roll(w, 1, 2) + pltpu.roll(w, lanes - 1, 2))
+
+
+def row_sum(w):
+    lanes = w[0].shape[1]
+    above = w[1:] + [pltpu.roll(w[0], 7, 0)]
+    below = [pltpu.roll(w[-1], 1, 0)] + w[:-1]
+    return [
+        (pltpu.roll(w[j], 1, 1) + pltpu.roll(w[j], lanes - 1, 1)) + (above[j] + below[j])
+        for j in range(len(w))
+    ]
 
 
 def kernel(slices, slabs, init_ref, fine_ref, sweep_ref, out_ref,
@@ -45,11 +55,18 @@
         {"space": above, "tm": other},
         {"space": below, "tm": other},
         {"tm": other},
-        {"tm": (pos + 2) % slices},
-        {"tm": (pos + slices - 2) % slices},
     )
     for peer in peers:
         pl.semaphore_signal(barrier, inc=1, device_id=peer, device_id_type=MESH)
+
+    @pl.when(chip > 0)
+    def _():
+        pl.semaphore_signal(barrier, inc=1, device_id={"tm": pos - 2}, device_id_type=MESH)
+
+    @pl.when(chip < chips - 1)
+    def _():
+        pl.semaphore_signal(barrier, inc=1, device_id={"tm": pos + 2}, device_id_type=MESH)
+
 
     fetch = pltpu.make_async_copy(init_ref.at[pl.ds(half * core, half)], fetched, fetch_sem)
     fetch.start()
@@ -142,12 +159,12 @@
         sweep_coef[power] = jnp.where(sweeps == power, factor, inner)
 
     def coarse(v):
-        power = v * ((1.0 + SLICE_TIME) - SLICE_TIME * (v * v))
-        total = sweep_coef[0] * power
+        power = [v[j] * ((1.0 + SLICE_TIME) - SLICE_TIME * (v[j] * v[j])) for j in range(rows)]
+        total = [sweep_coef[0] * x for x in power]
         for turn in range(SWEEPS):
-            power = planar_sum(power)
-            total = total + sweep_coef[turn + 1] * power
-        return total
+            power = row_sum(power)
+            total = [t + sweep_coef[turn + 1] * x for t, x in zip(total, power)]
+        return jnp.stack(total)
 
     def load(i, carry):
         for j in range(rows):
@@ -180,11 +197,8 @@
         return carry
 
     lax.fori_loop(0, half, deal, 0)
-    pl.semaphore_wait(barrier, len(peers))
-
-    def near(turn, i):
-        for piece in range(1 + turn):
-            halo(turn, 1 - core, piece, i).start()
+    ends = 1 - (chip + chips - 1) // chips + chip // (chips - 1)
+    pl.semaphore_wait(barrier, len(peers) + 2 - ends)
 
     def far(turn):
         def left(t, carry):
@@ -202,7 +216,7 @@
         lax.fori_loop(0, half, go, 0)
 
     def greet(t, carry):
-        near(0, half - 1 - t)
+        halo(0, 1 - core, 0, half - 1 - t).start()
         share(0, half - 1 - t).start()
         return carry
 
@@ -251,12 +265,15 @@
         def _():
             chain(turn, i).wait_recv()
 
+        if turn == 0:
+            halo(1, 1 - core, 0, i).start()
         g = coarse(state[1 + turn, 0, i])
         share_solved(turn, i).wait_recv()
         state[1 + turn, 1, i] = g + (solved[turn, 0, i] - kept[0, i])
         if turn == 0:
+            halo(1, 1 - core, 1, i).start()
+            share(1, i).start()
             kept[0, i] = g
-            share(1, i).start()
         g = coarse(state[1 + turn, 1, i])
         state[1 + turn, 2, i] = g + (solved[turn, 1, i] - kept[1, i])
 
@@ -266,7 +283,6 @@
 
         if turn == 0:
             kept[1, i] = g
-            near(1, i)
             level0[1, depth + mine(i)] = state[1, core, i]
         else:
             share_final(i).start()
@@ -280,9 +296,12 @@
             return carry
 
         lax.fori_loop(0, half, own, 0)
+        if turn == 1:
+            far(1)
         for d in range(2 - half, 1):
             diagonal(turn, d, half - 1 + d)
-        far(turn)
+        if turn == 0:
+            far(0)
         if turn == 0:
             intake(1)
         for d in range(1, half + 1):

time: 75.5 us -> 69.7 us (0.923); the launches traced: 74.2 us -> 69.6 us
  Pallas kernels: 71 us -> 66.4 us
    pallas_call x1, Pallas kernels: 71 us -> 66.4 us  [local(): pl.pallas_call(functools.partial(kernel, slices, slabs), out_shape=jax.Sh...]
where the time goes in v5:
time: 69.7 us; the launch traced here: 69.6 us
  Pallas kernels  66.4 us (95%)
  local copies, waits for them, and re-layouts  1.83 us (3%)
  between operations  1.31 us (2%)
    pallas_call x1, Pallas kernels, local(): pl.pallas_call(functools.partial(kernel, slices, slabs), out_shape=jax.Sh...  66.4 us
    unnamed x3, local copies, waits for them, and re-layouts  1.83 us

profile of v5, /device:TPU:225, one launch (start us, length us, event | category | flops | bytes accessed | tf_op | source)
XLA Modules:
  0.0 69.6 jit_solution(12742542737031368761)
XLA Ops:
  1.3 0.0 copy-start
  1.3 1.0 %copy-done = f32[8,128,128]{2,1,0:T(8,128)S(1)} copy-done((f32[8,128,128]{2,1,0:T(8,128)S(1)}, f32[8,128,128]{2,1,0:T(8,128)}, u32[]{:S(2)}) %copy-start) | copy-done | bytes 524312
  2.3 66.4 %shard_map.37 = f32[1,8,128,128]{3,2,1,0:T(8,128)S(1)} custom-call(f32[8,128,128]{2,1,0:T(8,128)S(1)} %copy-done, s32[1]{0:T(128)S(6)} %copy.5.fine_ref, s32[1]{0:T(128)S(6)} %copy.6.sweep_ref), custom_call_target="tpu_custom_call" | custom-call | tf_op jit(solution)/shard_map/pallas_call | solution.py:370
  68.8 0.8 %copy.7 = f32[1,8,128,128]{3,2,1,0:T(8,128)} copy(f32[1,8,128,128]{3,2,1,0:T(8,128)S(1)} %shard_map.37) | data formatting | bytes 1048576
Async XLA Ops:
  1.3 1.0 %copy-start = (f32[8,128,128]{2,1,0:T(8,128)S(1)}, f32[8,128,128]{2,1,0:T(8,128)}, u32[]{:S(2)}) copy-start(f32[8,128,128]{2,1,0:T(8,128)} %init_ref.1) | copy-start | bytes 1572868

commit v6 on v5

--- a/solution.py
+++ b/solution.py
@@ -267,7 +267,16 @@
 
         if turn == 0:
             halo(1, 1 - core, 0, i).start()
-        g = coarse(state[1 + turn, 0, i])
+
+        @pl.when(chip > 0)
+        def _():
+            state[1 + turn, 1, i] = coarse(state[1 + turn, 0, i])
+
+        @pl.when(chip == 0)
+        def _():
+            state[1 + turn, 1, i] = kept[0, i]
+
+        g = state[1 + turn, 1, i]
         share_solved(turn, i).wait_recv()
         state[1 + turn, 1, i] = g + (solved[turn, 0, i] - kept[0, i])
         if turn == 0:

time: 69.7 us -> 69.4 us (level)
  no operation moved by 1% of the time
where the time goes in v6:
time: 69.4 us; the launch traced here: 69.3 us
  Pallas kernels  66.2 us (95%)
  local copies, waits for them, and re-layouts  1.83 us (3%)
  between operations  1.31 us (2%)
    pallas_call x1, Pallas kernels, local(): pl.pallas_call(functools.partial(kernel, slices, slabs), out_shape=jax.Sh...  66.2 us
    unnamed x3, local copies, waits for them, and re-layouts  1.83 us

profile of v6, /device:TPU:225, one launch (start us, length us, event | category | flops | bytes accessed | tf_op | source)
XLA Modules:
  0.0 69.3 jit_solution(17628385398418875281)
XLA Ops:
  1.3 0.0 copy-start
  1.3 1.0 %copy-done = f32[8,128,128]{2,1,0:T(8,128)S(1)} copy-done((f32[8,128,128]{2,1,0:T(8,128)S(1)}, f32[8,128,128]{2,1,0:T(8,128)}, u32[]{:S(2)}) %copy-start) | copy-done | bytes 524312
  2.3 66.2 %shard_map.37 = f32[1,8,128,128]{3,2,1,0:T(8,128)S(1)} custom-call(f32[8,128,128]{2,1,0:T(8,128)S(1)} %copy-done, s32[1]{0:T(128)S(6)} %copy.5.fine_ref, s32[1]{0:T(128)S(6)} %copy.6.sweep_ref), custom_call_target="tpu_custom_call" | custom-call | tf_op jit(solution)/shard_map/pallas_call | solution.py:379
  68.5 0.8 %copy.7 = f32[1,8,128,128]{3,2,1,0:T(8,128)} copy(f32[1,8,128,128]{3,2,1,0:T(8,128)S(1)} %shard_map.37) | data formatting | bytes 1048576
Async XLA Ops:
  1.3 1.0 %copy-start = (f32[8,128,128]{2,1,0:T(8,128)S(1)}, f32[8,128,128]{2,1,0:T(8,128)}, u32[]{:S(2)}) copy-start(f32[8,128,128]{2,1,0:T(8,128)} %init_ref.1) | copy-start | bytes 1572868
